TPU v7x, 512 devices: a whole 4x8x8 slice. The times are simulated.
512 devices in a mesh: grp: 8 (over x, core), blk: 64 (over y, z).
Axes of the slice: x: 4, y: 8, z: 8, core: 2. Of those that a mesh axis runs over, the one named last changes fastest.
Arguments:
- features: bfloat16 [65536, 256], P(('grp', 'blk')), may hold values from -6 to 6
- dest: int32 [65536, 1], P(('grp', 'blk')), may hold values from 0 to 63; in each aligned block of 128 rows (0 to 127, 128 to 255, ...) at most 4 rows name the same one
- placement: int32 [512, 256], P(('grp', 'blk')), may hold values from 0 to 255, each once within a row
- weight: bfloat16 [27, 256, 128], replicated, may hold values from -0.078125 to 0.078125
- grad_out: bfloat16 [64, 512, 4, 128], P('grp', 'blk'), may hold values from -6 to 6
Outputs:
- output: bfloat16 [64, 512, 4, 128], P('grp', 'blk')
- grad_rows: bfloat16 [65536, 256], P(('grp', 'blk'))
- weight_grad: bfloat16 [27, 256, 128], replicated
Inputs may be any that keep to these rules, and one draw needn't show every extreme that they name: `dest`: among the rows of one device no value is named by more than 4 rows, a bound that some block reaches. `placement`: each row is a permutation of 0 to 255.
All inputs are finite; a program needn't handle non-finite values.
Results may differ from a plain program's by a relative error of at most 0.0013.
Values may be sent and summed in bfloat16 or wider, within the bound.
A program may use at most 64 MiB of HBM per device.

v0:
```python
import math
import jax
import jax.numpy as jnp
from jax import lax
from jax.sharding import PartitionSpec as P


def extended(cells, sides, width):
    for axis, dim in sides:
        count = lax.axis_size(axis)
        ends = count - 1
        head = lax.slice_in_dim(cells, 0, width, axis=dim)
        tail = lax.slice_in_dim(cells, cells.shape[dim] - width, cells.shape[dim], axis=dim)
        cells = jnp.concatenate(
            [
                lax.ppermute(tail, axis, [(i, (i + 1) % count) for i in range(ends)]),
                cells,
                lax.ppermute(head, axis, [((i + 1) % count, i) for i in range(ends)]),
            ],
            axis=dim,
        )
    return cells


def shards(features, dest, placement, weight, grad_out):
    row_count, channels = features.shape
    blk_count = lax.axis_size("blk")
    grp_count = lax.axis_size("grp")
    voxel_of_slot = placement[0]
    voxel_count = voxel_of_slot.shape[0]
    capacity = voxel_count // blk_count
    size_x, size_y, size_z, out_channels = grad_out.shape
    target = dest[:, 0]
    owners = jnp.arange(blk_count, dtype=jnp.int32)
    one_hot = (target[:, None] == owners[None, :]).astype(jnp.int32)
    slot_rank = jnp.sum((jnp.cumsum(one_hot, axis=0) - one_hot) * one_hot, axis=1)
    send_counts = jnp.sum(one_hot, axis=0).reshape(blk_count, 1)
    slot_index = target * capacity + slot_rank
    outgoing = jnp.zeros((voxel_count, channels), jnp.bfloat16).at[slot_index].set(features)
    incoming, recv_counts = (
        lax.all_to_all(
            outgoing.reshape(blk_count, capacity, channels),
            "blk",
            split_axis=0,
            concat_axis=0,
            tiled=True,
        ),
        lax.all_to_all(send_counts, "blk", split_axis=0, concat_axis=0, tiled=True),
    )
    filled = (
        (jnp.arange(capacity, dtype=jnp.int32)[None, :] < recv_counts)
        .reshape(-1)
        .astype(jnp.float32)
    )
    voxel_rows = (
        jnp.zeros((voxel_count, channels), jnp.bfloat16)
        .at[voxel_of_slot]
        .set(incoming.reshape(voxel_count, channels))
    )
    occupied = jnp.zeros((voxel_count,), jnp.float32).at[voxel_of_slot].set(filled)[:, None]
    voxel_grid = voxel_rows.reshape(size_x, size_y, size_z, channels)
    padded = extended(voxel_grid, (("grp", 0), ("blk", 1)), 1)
    padded = jnp.pad(padded, ((0, 0), (0, 0), (1, 1), (0, 0)))
    shifted = []
    total = jnp.zeros((voxel_count, out_channels), jnp.float32)
    for offset in range(27):
        shift_x, shift_y, shift_z = (offset // 9, offset // 3 % 3, offset % 3)
        window = padded[
            shift_x : shift_x + size_x, shift_y : shift_y + size_y, shift_z : shift_z + size_z
        ].reshape(voxel_count, channels)
        shifted.append(window)
        total = total + jnp.dot(window, weight[offset], preferred_element_type=jnp.float32)
    output = (total * occupied).astype(jnp.bfloat16).reshape(size_x, size_y, size_z, out_channels)
    masked_grad = (
        grad_out.reshape(voxel_count, out_channels).astype(jnp.float32) * occupied
    ).astype(jnp.bfloat16)
    grad_padded = extended(
        masked_grad.reshape(size_x, size_y, size_z, out_channels), (("grp", 0), ("blk", 1)), 1
    )
    grad_padded = jnp.pad(grad_padded, ((0, 0), (0, 0), (1, 1), (0, 0)))
    back_total = jnp.zeros((voxel_count, channels), jnp.float32)
    partials = []
    for offset in range(27):
        shift_x, shift_y, shift_z = (offset // 9, offset // 3 % 3, offset % 3)
        window = grad_padded[
            2 - shift_x : 2 - shift_x + size_x,
            2 - shift_y : 2 - shift_y + size_y,
            2 - shift_z : 2 - shift_z + size_z,
        ].reshape(voxel_count, out_channels)
        back_total = back_total + lax.dot_general(
            window, weight[offset], (((1,), (1,)), ((), ())), preferred_element_type=jnp.float32
        )
        partials.append(
            lax.dot_general(
                shifted[offset],
                masked_grad,
                (((0,), (0,)), ((), ())),
                preferred_element_type=jnp.float32,
            )
        )
    grad_grid = (back_total * occupied).astype(jnp.bfloat16)
    weight_terms = jnp.stack(partials).reshape(27 * channels, out_channels)
    grad_scale = 1.0 / math.sqrt(row_count * blk_count * grp_count)
    weight_grad = (lax.psum(weight_terms, ("grp", "blk")) * grad_scale).astype(jnp.bfloat16)
    weight_grad = weight_grad.reshape(27, channels, out_channels)
    returning = grad_grid[voxel_of_slot].reshape(blk_count, capacity, channels)
    returned = lax.all_to_all(returning, "blk", split_axis=0, concat_axis=0, tiled=True)
    grad_rows = returned.reshape(voxel_count, channels)[slot_index]
    return (output, grad_rows, weight_grad)


def solution(mesh):
    in_specs = (
        P(("grp", "blk"), None),
        P(("grp", "blk"), None),
        P(("grp", "blk"), None),
        P(),
        P("grp", "blk", None, None),
    )
    out_specs = (P("grp", "blk", None, None), P(("grp", "blk"), None), P())
    return jax.shard_map(shards, mesh=mesh, in_specs=in_specs, out_specs=out_specs, check_vma=False)
```

profile of v0, /device:TPU:24, one launch (start us, length us, event | category | flops | bytes accessed | tf_op | source)
XLA Modules:
  0.0 480.3 jit_solution(8768574311076272875)
XLA Ops:
  9.6 16.4 %all-to-all-start.1 = ((s32[64,1,1]{2,1,0:T(1,128)}), s32[64,1,1]{2,1,0:T(1,128)S(1)}, u32[]{:S(2)}, u32[]{:S(2)}) async-start(s32[64,1,1]{2,1,0:T(1,128)} %copy.183), calls=%async_computation.1 | async-start | bytes 65536 | tf_op jit(solution)/shard_map/all_to_all | solution.py:48
  29.5 5.8 %all-to-all-done.1 = s32[64,1,1]{2,1,0:T(1,128)S(1)} async-done(((s32[64,1,1]{2,1,0:T(1,128)}), s32[64,1,1]{2,1,0:T(1,128)S(1)}, u32[]{:S(2)}, u32[]{:S(2)}) %all-to-all-start.1) | async-done | bytes 288 | tf_op jit(solution)/shard_map/all_to_all | solution.py:48
  35.3 7.3 %all-to-all-start = ((bf16[64,4,256]{2,1,0:T(4,128)(2,1)}), bf16[64,4,256]{2,1,0:T(4,128)(2,1)S(1)}, u32[]{:S(2)}, u32[]{:S(2)}) async-start(bf16[64,4,256]{2,1,0:T(4,128)(2,1)} %reshape.379), calls=%async_computation | async-start | bytes 262144 | tf_op jit(solution)/shard_map/all_to_all | solution.py:41
  44.0 1.4 scatter_custom_fusion.2
  47.8 3.0 collective-permute-start.4
  51.8 3.4 collective-permute-start.6
  55.2 4.6 collective-permute-start.7
  67.1 1.5 scatter_custom_fusion.1
  68.6 1.9 collective-permute-start
  72.5 12.3 %all-to-all-start.2 = ((bf16[64,4,256]{2,1,0:T(4,128)(2,1)}), bf16[64,4,256]{2,1,0:T(4,128)(2,1)S(1)}, u32[]{:S(2)}, u32[]{:S(2)}) async-start(bf16[64,4,256]{2,1,0:T(4,128)(2,1)} %reshape.436), calls=%async_computation.2 | async-start | bytes 262144 | tf_op jit(solution)/shard_map/all_to_all | solution.py:107
  86.4 4.1 collective-permute-done.1
  90.6 3.4 collective-permute-start.2
  93.9 4.8 collective-permute-start.3
  99.7 1.5 gather_fusion.1
  102.0 1.5 fusion.215
  111.5 1.6 copy.174
  119.0 1.6 copy.176
  120.6 1.6 reshape.402
  122.2 1.6 copy.175
  123.8 1.6 reshape.401
  125.4 1.6 copy.173
  127.0 1.6 reshape.399
  128.6 1.6 copy.172
  130.2 1.6 reshape.398
  131.8 1.6 copy.170
  133.4 1.6 reshape.396
  135.0 1.6 copy.169
  136.6 1.6 reshape.395
  138.2 1.6 copy.168
  139.8 1.6 reshape.394
  141.4 1.6 copy.167
  143.0 1.6 reshape.393
  144.6 1.6 copy.165
  146.2 1.6 reshape.391
  147.8 1.6 copy.164
  149.4 1.6 reshape.390
  151.0 1.6 copy.162
  152.6 1.6 reshape.388
  154.9 1.6 reshape.387
  156.5 1.6 copy.158
  158.2 1.6 reshape.385
  159.7 1.6 copy.157
  161.3 1.6 reshape.384
  163.0 1.6 copy.155
  164.6 1.6 reshape.382
  182.7 1.8 copy-done.2
  188.6 281.5 %all-reduce.4.cloned.1.call-done = f32[6912,128]{1,0:T(8,128)} async-done(((f32[6912,128]{1,0:T(8,128)}), f32[6912,128]{1,0:T(8,128)}) %all-reduce.4.cloned.1.call-update) | async-done | bytes 3538960 | tf_op jit(solution)/shard_map/psum | solution.py:104
  470.1 3.4 multiply_convert_fusion
  (222 shorter events, 57.6 us)
Async XLA Ops:
  9.6 25.6 %all-to-all-start.1 = ((s32[64,1,1]{2,1,0:T(1,128)}), s32[64,1,1]{2,1,0:T(1,128)S(1)}, u32[]{:S(2)}, u32[]{:S(2)}) async-start(s32[64,1,1]{2,1,0:T(1,128)} %copy.183), calls=%async_computation.1 | async-start | bytes 65536 | tf_op jit(solution)/shard_map/all_to_all | solution.py:48
  35.3 31.7 %all-to-all-start = ((bf16[64,4,256]{2,1,0:T(4,128)(2,1)}), bf16[64,4,256]{2,1,0:T(4,128)(2,1)S(1)}, u32[]{:S(2)}, u32[]{:S(2)}) async-start(bf16[64,4,256]{2,1,0:T(4,128)(2,1)} %reshape.379), calls=%async_computation | async-start | bytes 262144 | tf_op jit(solution)/shard_map/all_to_all | solution.py:41
  42.6 19.2 %copy-start = (bf16[27,256,128]{2,1,0:T(8,128)(2,1)S(1)}, bf16[27,256,128]{2,1,0:T(8,128)(2,1)}, u32[]{:S(2)}) copy-start(bf16[27,256,128]{2,1,0:T(8,128)(2,1)} %param.8) | copy-start | bytes 5308420
  46.5 5.3 %collective-permute-start.5 = (bf16[1,8,4,128]{3,2,1,0:T(4,128)(2,1)S(1)}, bf16[1,8,4,128]{3,2,1,0:T(4,128)(2,1)S(1)}, u32[]{:S(2)}, u32[]{:S(2)}) collective-permute-start(bf16[1,8,4,128]{3,2,1,0:T(4,128)(2,1)S(1)} %bitcast.495), channel_id=1, source_target_pairs={{64,0},{128,64},{192,128},{256,192},{320,256},{384,320},{448,384},... | collective-permute-start | bytes 24584 | tf_op jit(solution)/shard_map/ppermute | solution.py:18
  47.8 4.0 collective-permute-start.4
  51.8 8.0 %collective-permute-start.6 = (bf16[10,1,4,128]{3,2,1,0:T(4,128)(2,1)S(1)}, bf16[10,1,4,128]{3,2,1,0:T(4,128)(2,1)S(1)}, u32[]{:S(2)}, u32[]{:S(2)}) collective-permute-start(bf16[10,1,4,128]{3,2,1,0:T(4,128)(2,1)S(1)} %get-tuple-element.65), channel_id=1, source_target_pairs={{0,1},{1,2},{2,3},{3,4},{4,5},{5,6},{6,7},{7,8},{8,9},{9,10},{10,1... | collective-permute-start | bytes 30728 | tf_op jit(solution)/shard_map/ppermute | solution.py:16
  55.2 5.9 %collective-permute-start.7 = (bf16[10,1,4,128]{3,2,1,0:T(4,128)(2,1)S(1)}, bf16[10,1,4,128]{3,2,1,0:T(4,128)(2,1)S(1)}, u32[]{:S(2)}, u32[]{:S(2)}) collective-permute-start(bf16[10,1,4,128]{3,2,1,0:T(4,128)(2,1)S(1)} %get-tuple-element.66), channel_id=1, source_target_pairs={{1,0},{2,1},{3,2},{4,3},{5,4},{6,5},{7,6},{8,7},{9,8},{10,9},{11,1... | collective-permute-start | bytes 30728 | tf_op jit(solution)/shard_map/ppermute | solution.py:18
  68.6 17.7 %collective-permute-start = (bf16[1,8,4,256]{3,1,2,0:T(8,128)(2,1)S(1)}, bf16[1,8,4,256]{3,1,2,0:T(8,128)(2,1)S(1)}, u32[]{:S(2)}, u32[]{:S(2)}) collective-permute-start(bf16[1,8,4,256]{3,1,2,0:T(8,128)(2,1)S(1)} %copy.152), channel_id=1, source_target_pairs={{0,64},{64,128},{128,192},{192,256},{256,320},{320,384},{384,448},... | collective-permute-start | bytes 49160 | tf_op jit(solution)/shard_map/ppermute | solution.py:16
  72.5 27.1 %all-to-all-start.2 = ((bf16[64,4,256]{2,1,0:T(4,128)(2,1)}), bf16[64,4,256]{2,1,0:T(4,128)(2,1)S(1)}, u32[]{:S(2)}, u32[]{:S(2)}) async-start(bf16[64,4,256]{2,1,0:T(4,128)(2,1)} %reshape.436), calls=%async_computation.2 | async-start | bytes 262144 | tf_op jit(solution)/shard_map/all_to_all | solution.py:107
  84.9 385.2 %all-reduce.4.cloned.1.call-start = ((), (), s32[]{:S(2)}) async-start(), calls=%async_computation.3 | async-start | bytes 7077888 | tf_op jit(solution)/shard_map/psum | solution.py:104
  85.0 13.8 %copy-start.18 = (bf16[8,8,4,256]{3,2,1,0:T(4,128)(2,1)}, bf16[8,8,4,256]{3,2,1,0:T(4,128)(2,1)S(1)}, u32[]{:S(2)}) copy-start(bf16[8,8,4,256]{3,2,1,0:T(4,128)(2,1)S(1)} %reshape.381) | copy-start | bytes 393220
  85.0 5.5 %collective-permute-start.1 = (bf16[1,8,4,256]{3,1,2,0:T(8,128)(2,1)S(1)}, bf16[1,8,4,256]{3,1,2,0:T(8,128)(2,1)S(1)}, u32[]{:S(2)}, u32[]{:S(2)}) collective-permute-start(bf16[1,8,4,256]{3,1,2,0:T(8,128)(2,1)S(1)} %copy.153), channel_id=1, source_target_pairs={{64,0},{128,64},{192,128},{256,192},{320,256},{384,320},{448,384},... | collective-permute-start | bytes 49160 | tf_op jit(solution)/shard_map/ppermute | solution.py:18
  86.4 14.8 %copy-start.31 = (bf16[9,8,4,256]{3,1,2,0:T(8,128)(2,1)}, bf16[9,8,4,256]{3,1,2,0:T(8,128)(2,1)S(1)}, u32[]{:S(2)}) copy-start(bf16[9,8,4,256]{3,1,2,0:T(8,128)(2,1)S(1)} %get-tuple-element.53) | copy-start | bytes 442372
  90.5 8.3 %copy-start.27 = (bf16[9,8,4,256]{3,1,2,0:T(8,128)(2,1)}, bf16[9,8,4,256]{3,1,2,0:T(8,128)(2,1)S(1)}, u32[]{:S(2)}) copy-start(bf16[9,8,4,256]{3,1,2,0:T(8,128)(2,1)S(1)} %get-tuple-element.71) | copy-start | bytes 442372
  90.6 10.6 %collective-permute-start.2 = (bf16[10,1,4,256]{3,1,2,0:T(2,128)(2,1)S(1)}, bf16[10,1,4,256]{3,1,2,0:T(2,128)(2,1)S(1)}, u32[]{:S(2)}, u32[]{:S(2)}) collective-permute-start(bf16[10,1,4,256]{3,1,2,0:T(2,128)(2,1)S(1)} %get-tuple-element.50), channel_id=1, source_target_pairs={{0,1},{1,2},{2,3},{3,4},{4,5},{5,6},{6,7},{7,8},{8,9},{9,10},{10,1... | collective-permute-start | bytes 61448 | tf_op jit(solution)/shard_map/ppermute | solution.py:16
  93.9 7.2 %collective-permute-start.3 = (bf16[10,1,4,256]{3,1,2,0:T(2,128)(2,1)S(1)}, bf16[10,1,4,256]{3,1,2,0:T(2,128)(2,1)S(1)}, u32[]{:S(2)}, u32[]{:S(2)}) collective-permute-start(bf16[10,1,4,256]{3,1,2,0:T(2,128)(2,1)S(1)} %get-tuple-element.51), channel_id=1, source_target_pairs={{1,0},{2,1},{3,2},{4,3},{5,4},{6,5},{7,6},{8,7},{9,8},{10,9},{11,1... | collective-permute-start | bytes 61448 | tf_op jit(solution)/shard_map/ppermute | solution.py:18
  101.2 0.6 copy-start.29
  103.5 0.9 copy-start.30
  105.5 1.8 copy-start.20
  154.9 15.8 %copy-start.8 = (bf16[256,256]{1,0:T(8,128)(2,1)S(1)}, bf16[256,256]{1,0:T(8,128)(2,1)}, u32[]{:S(2)}) copy-start(bf16[256,256]{1,0:T(8,128)(2,1)} %reshape.386) | copy-start | bytes 393220
  166.2 4.7 copy-start.17
  166.2 4.9 %copy-start.16 = (bf16[256,256]{1,0:T(8,128)(2,1)S(1)}, bf16[256,256]{1,0:T(8,128)(2,1)}, u32[]{:S(2)}) copy-start(bf16[256,256]{1,0:T(8,128)(2,1)} %reshape.388) | copy-start | bytes 393220
  166.2 5.1 %copy-start.11 = (bf16[256,256]{1,0:T(8,128)(2,1)S(1)}, bf16[256,256]{1,0:T(8,128)(2,1)}, u32[]{:S(2)}) copy-start(bf16[256,256]{1,0:T(8,128)(2,1)} %reshape.389) | copy-start | bytes 393220
  166.2 5.3 %copy-start.15 = (bf16[256,256]{1,0:T(8,128)(2,1)S(1)}, bf16[256,256]{1,0:T(8,128)(2,1)}, u32[]{:S(2)}) copy-start(bf16[256,256]{1,0:T(8,128)(2,1)} %reshape.390) | copy-start | bytes 393220
  167.3 4.3 copy-start.14
  168.4 3.4 copy-start.10
  169.5 2.5 copy-start.13
  170.7 1.5 copy-start.12
  170.9 1.7 copy-start.26
  171.1 2.0 copy-start.1
  173.3 0.9 copy-start.32
  174.5 0.9 copy-start.25
  175.6 0.9 copy-start.24
  176.7 0.9 copy-start.19
  177.9 0.9 copy-start.23
  179.0 0.9 copy-start.22
  180.2 0.9 copy-start.28
  181.3 0.9 copy-start.21
  182.7 1.8 copy-start.2
  184.5 0.9 copy-start.9
  184.5 1.1 copy-start.7
  184.5 1.4 copy-start.6
  185.4 0.9 copy-start.5
  185.4 1.3 copy-start.4
  185.4 1.5 copy-start.3
Sparse Core Ops, SparseCore 0:
  184.6 285.4 all-reduce.3
where the time goes:
time: 482 us; the launch traced here: 480 us
  waiting for transfers between devices  293 us (61%)
  local copies, waits for them, and re-layouts  80.7 us (17%)
  starting transfers between devices  59.6 us (12%)
  matrix products  20.7 us (4%)
  between operations  15.2 us (3%)
  other arithmetic  11.4 us (2%)
    psum x1, waiting for transfers between devices, shards(): lax.psum(weight_terms, ('grp', 'blk')) * grad_scale  282 us
    slice x29, local copies, waits for them, and re-layouts, shards(): padded[shift_x:shift_x + size_x, shift_y:shift_y + size_y, shift_z:shift_...  32.4 us
    reshape x26, local copies, waits for them, and re-layouts, shards(): window = padded[shift_x:shift_x + size_x, shift_y:shift_y + size_y, shift...  30.6 us
    all_to_all x1, starting transfers between devices, shards(): lax.all_to_all(send_counts, 'blk', split_axis=0, concat_axis=0, tiled=True)  16.4 us
    all_to_all x1, starting transfers between devices, shards(): lax.all_to_all(returning, 'blk', split_axis=0, concat_axis=0, tiled=True)  12.3 us
    ppermute x4, starting transfers between devices, extended(): lax.ppermute(head, axis, [((i + 1) % count, i) for i in range(ends)])  11.9 us
    ppermute x4, starting transfers between devices, extended(): lax.ppermute(tail, axis, [(i, (i + 1) % count) for i in range(ends)])  11.7 us
  transfers between devices with their start and end apart: 12, of which 4 were waited for; matrix products, arithmetic and copies ran while one was open for 4% of the time, Pallas kernels for 0%

commit v1 on v0

--- a/solution.py
+++ b/solution.py
@@ -3,6 +3,11 @@
 import jax.numpy as jnp
 from jax import lax
 from jax.sharding import PartitionSpec as P
+
+
+def one_after_other(x, first, second):
+    half = lax.psum(x, first)
+    return lax.psum(half, second)
 
 
 def extended(cells, sides, width):
@@ -101,7 +106,7 @@
     grad_grid = (back_total * occupied).astype(jnp.bfloat16)
     weight_terms = jnp.stack(partials).reshape(27 * channels, out_channels)
     grad_scale = 1.0 / math.sqrt(row_count * blk_count * grp_count)
-    weight_grad = (lax.psum(weight_terms, ("grp", "blk")) * grad_scale).astype(jnp.bfloat16)
+    weight_grad = (one_after_other(weight_terms, "grp", "blk") * grad_scale).astype(jnp.bfloat16)
     weight_grad = weight_grad.reshape(27, channels, out_channels)
     returning = grad_grid[voxel_of_slot].reshape(blk_count, capacity, channels)
     returned = lax.all_to_all(returning, "blk", split_axis=0, concat_axis=0, tiled=True)

time: 482 us -> 431 us (0.89)
  the two profiles are of different devices: /device:TPU:24 before, /device:TPU:2 now
where the time goes in v1:
time: 431 us; the launch traced here: 429 us
  waiting for transfers between devices  239 us (55%)
  local copies, waits for them, and re-layouts  68.4 us (16%)
  starting transfers between devices  53.2 us (12%)
  matrix products  42.2 us (10%)
  between operations  15.1 us (4%)
  other arithmetic  11.4 us (3%)
    psum x1, waiting for transfers between devices, one_after_other(): return lax.psum(half, second)  146 us
    psum x1, waiting for transfers between devices, one_after_other(): half = lax.psum(x, first)  74.8 us
    reshape x26, local copies, waits for them, and re-layouts, shards(): window = padded[shift_x:shift_x + size_x, shift_y:shift_y + size_y, shift...  29 us
    slice x29, local copies, waits for them, and re-layouts, shards(): padded[shift_x:shift_x + size_x, shift_y:shift_y + size_y, shift_z:shift_...  27.4 us
    dot_general x27, matrix products, shards(): lax.dot_general(shifted[offset], masked_grad, (((0,), (0,)), ((), ())), p...  24.7 us
    all_to_all x1, starting transfers between devices, shards(): lax.all_to_all(send_counts, 'blk', split_axis=0, concat_axis=0, tiled=True)  16.6 us
    all_to_all x1, starting transfers between devices, shards(): lax.all_to_all(returning, 'blk', split_axis=0, concat_axis=0, tiled=True)  13 us
    dot_general x27, matrix products, shards(): jnp.dot(window, weight[offset], preferred_element_type=jnp.float32)  12.5 us
  transfers between devices with their start and end apart: 13, of which 7 were waited for; matrix products, arithmetic and copies ran while one was open for 12% of the time, Pallas kernels for 0%

profile of v1, /device:TPU:2, one launch (start us, length us, event | category | flops | bytes accessed | tf_op | source)
XLA Modules:
  0.0 429.4 jit_solution(12504599183733194274)
XLA Ops:
  9.6 16.6 %all-to-all-start.1 = ((s32[64,1,1]{2,1,0:T(1,128)}), s32[64,1,1]{2,1,0:T(1,128)S(1)}, u32[]{:S(2)}, u32[]{:S(2)}) async-start(s32[64,1,1]{2,1,0:T(1,128)} %copy.183), calls=%async_computation.1 | async-start | bytes 65536 | tf_op jit(solution)/shard_map/all_to_all | solution.py:53
  29.7 8.5 %all-to-all-done.1 = s32[64,1,1]{2,1,0:T(1,128)S(1)} async-done(((s32[64,1,1]{2,1,0:T(1,128)}), s32[64,1,1]{2,1,0:T(1,128)S(1)}, u32[]{:S(2)}, u32[]{:S(2)}) %all-to-all-start.1) | async-done | bytes 288 | tf_op jit(solution)/shard_map/all_to_all | solution.py:53
  38.1 4.6 %all-to-all-start = ((bf16[64,4,256]{2,1,0:T(4,128)(2,1)}), bf16[64,4,256]{2,1,0:T(4,128)(2,1)S(1)}, u32[]{:S(2)}, u32[]{:S(2)}) async-start(bf16[64,4,256]{2,1,0:T(4,128)(2,1)} %reshape.379), calls=%async_computation | async-start | bytes 262144 | tf_op jit(solution)/shard_map/all_to_all | solution.py:46
  46.7 1.9 collective-permute-start.5
  48.6 2.4 collective-permute-start.4
  52.0 1.6 collective-permute-done.4
  53.6 3.4 collective-permute-start.6
  58.3 4.2 collective-permute-done.7
  68.4 1.5 scatter_custom_fusion.1
  69.9 1.9 collective-permute-start
  73.9 13.0 %all-to-all-start.2 = ((bf16[64,4,256]{2,1,0:T(4,128)(2,1)}), bf16[64,4,256]{2,1,0:T(4,128)(2,1)S(1)}, u32[]{:S(2)}, u32[]{:S(2)}) async-start(bf16[64,4,256]{2,1,0:T(4,128)(2,1)} %reshape.436), calls=%async_computation.2 | async-start | bytes 262144 | tf_op jit(solution)/shard_map/all_to_all | solution.py:112
  87.1 3.4 collective-permute-start.1
  91.9 3.2 collective-permute-start.2
  97.5 2.4 all-to-all-done.2
  100.0 1.5 gather_fusion.1
  102.9 1.5 fusion.215
  107.8 1.6 copy.166
  110.4 1.6 copy.156
  112.0 1.6 reshape.383
  113.6 1.6 copy.167
  115.2 1.6 reshape.393
  116.8 1.6 copy.165
  118.4 1.6 reshape.391
  120.0 1.6 copy.164
  121.7 1.6 reshape.390
  123.2 1.6 copy.162
  124.9 1.6 reshape.388
  126.5 1.6 copy.161
  128.1 1.6 reshape.387
  129.7 1.6 copy.158
  131.3 1.6 reshape.385
  132.9 1.6 copy.157
  134.5 1.6 reshape.384
  136.1 1.6 copy.155
  137.7 1.6 reshape.382
  139.3 1.7 fusion.105
  141.0 1.8 fusion.29
  169.8 74.8 %all-reduce.5.cloned.1.call-done = f32[6912,128]{1,0:T(8,128)} async-done(((f32[6912,128]{1,0:T(8,128)}), f32[6912,128]{1,0:T(8,128)}) %all-reduce.5.cloned.1.call-update) | async-done | bytes 3538960 | tf_op jit(solution)/shard_map/psum | solution.py:9
  245.8 1.6 copy.181
  247.5 1.6 copy.171
  249.1 1.6 copy.174
  251.6 1.6 reshape.397
  253.2 1.6 reshape.400
  254.8 1.6 copy.182
  256.4 1.6 reshape.407
  262.1 1.6 reshape.402
  272.9 146.2 %all-reduce.7.cloned.1.call-done = f32[6912,128]{1,0:T(8,128)} async-done(((f32[6912,128]{1,0:T(8,128)}), f32[6912,128]{1,0:T(8,128)}) %all-reduce.7.cloned.1.call-update) | async-done | bytes 3538960 | tf_op jit(solution)/shard_map/psum | solution.py:10
  419.2 3.4 multiply_convert_fusion
  (221 shorter events, 71.4 us)
Async XLA Ops:
  9.6 28.5 %all-to-all-start.1 = ((s32[64,1,1]{2,1,0:T(1,128)}), s32[64,1,1]{2,1,0:T(1,128)S(1)}, u32[]{:S(2)}, u32[]{:S(2)}) async-start(s32[64,1,1]{2,1,0:T(1,128)} %copy.183), calls=%async_computation.1 | async-start | bytes 65536 | tf_op jit(solution)/shard_map/all_to_all | solution.py:53
  38.1 30.2 %all-to-all-start = ((bf16[64,4,256]{2,1,0:T(4,128)(2,1)}), bf16[64,4,256]{2,1,0:T(4,128)(2,1)S(1)}, u32[]{:S(2)}, u32[]{:S(2)}) async-start(bf16[64,4,256]{2,1,0:T(4,128)(2,1)} %reshape.379), calls=%async_computation | async-start | bytes 262144 | tf_op jit(solution)/shard_map/all_to_all | solution.py:46
  42.7 20.3 %copy-start = (bf16[27,256,128]{2,1,0:T(8,128)(2,1)S(1)}, bf16[27,256,128]{2,1,0:T(8,128)(2,1)}, u32[]{:S(2)}) copy-start(bf16[27,256,128]{2,1,0:T(8,128)(2,1)} %param.8) | copy-start | bytes 5308420
  46.7 5.3 %collective-permute-start.5 = (bf16[1,8,4,128]{3,2,1,0:T(4,128)(2,1)S(1)}, bf16[1,8,4,128]{3,2,1,0:T(4,128)(2,1)S(1)}, u32[]{:S(2)}, u32[]{:S(2)}) collective-permute-start(bf16[1,8,4,128]{3,2,1,0:T(4,128)(2,1)S(1)} %bitcast.495), channel_id=1, source_target_pairs={{64,0},{128,64},{192,128},{256,192},{320,256},{384,320},{448,384},... | collective-permute-start | bytes 24584 | tf_op jit(solution)/shard_map/ppermute | solution.py:23
  48.6 5.0 %collective-permute-start.4 = (bf16[1,8,4,128]{3,2,1,0:T(4,128)(2,1)S(1)}, bf16[1,8,4,128]{3,2,1,0:T(4,128)(2,1)S(1)}, u32[]{:S(2)}, u32[]{:S(2)}) collective-permute-start(bf16[1,8,4,128]{3,2,1,0:T(4,128)(2,1)S(1)} %bitcast.494), channel_id=1, source_target_pairs={{0,64},{64,128},{128,192},{192,256},{256,320},{320,384},{384,448},... | collective-permute-start | bytes 24584 | tf_op jit(solution)/shard_map/ppermute | solution.py:21
  53.6 4.7 %collective-permute-start.6 = (bf16[10,1,4,128]{3,2,1,0:T(4,128)(2,1)S(1)}, bf16[10,1,4,128]{3,2,1,0:T(4,128)(2,1)S(1)}, u32[]{:S(2)}, u32[]{:S(2)}) collective-permute-start(bf16[10,1,4,128]{3,2,1,0:T(4,128)(2,1)S(1)} %get-tuple-element.65), channel_id=1, source_target_pairs={{0,1},{1,2},{2,3},{3,4},{4,5},{5,6},{6,7},{7,8},{8,9},{9,10},{10,1... | collective-permute-start | bytes 30728 | tf_op jit(solution)/shard_map/ppermute | solution.py:21
  56.9 5.6 %collective-permute-start.7 = (bf16[10,1,4,128]{3,2,1,0:T(4,128)(2,1)S(1)}, bf16[10,1,4,128]{3,2,1,0:T(4,128)(2,1)S(1)}, u32[]{:S(2)}, u32[]{:S(2)}) collective-permute-start(bf16[10,1,4,128]{3,2,1,0:T(4,128)(2,1)S(1)} %get-tuple-element.66), channel_id=1, source_target_pairs={{1,0},{2,1},{3,2},{4,3},{5,4},{6,5},{7,6},{8,7},{9,8},{10,9},{11,1... | collective-permute-start | bytes 30728 | tf_op jit(solution)/shard_map/ppermute | solution.py:23
  69.9 20.5 %collective-permute-start = (bf16[1,8,4,256]{3,1,2,0:T(8,128)(2,1)S(1)}, bf16[1,8,4,256]{3,1,2,0:T(8,128)(2,1)S(1)}, u32[]{:S(2)}, u32[]{:S(2)}) collective-permute-start(bf16[1,8,4,256]{3,1,2,0:T(8,128)(2,1)S(1)} %copy.152), channel_id=1, source_target_pairs={{0,64},{64,128},{128,192},{192,256},{256,320},{320,384},{384,448},... | collective-permute-start | bytes 49160 | tf_op jit(solution)/shard_map/ppermute | solution.py:21
  73.9 26.1 %all-to-all-start.2 = ((bf16[64,4,256]{2,1,0:T(4,128)(2,1)}), bf16[64,4,256]{2,1,0:T(4,128)(2,1)S(1)}, u32[]{:S(2)}, u32[]{:S(2)}) async-start(bf16[64,4,256]{2,1,0:T(4,128)(2,1)} %reshape.436), calls=%async_computation.2 | async-start | bytes 262144 | tf_op jit(solution)/shard_map/all_to_all | solution.py:112
  86.9 157.7 %all-reduce.5.cloned.1.call-start = ((), (), s32[]{:S(2)}) async-start(), calls=%async_computation.3 | async-start | bytes 7077888 | tf_op jit(solution)/shard_map/psum | solution.py:9
  87.0 9.6 %copy-start.15 = (bf16[8,8,4,256]{3,2,1,0:T(4,128)(2,1)}, bf16[8,8,4,256]{3,2,1,0:T(4,128)(2,1)S(1)}, u32[]{:S(2)}) copy-start(bf16[8,8,4,256]{3,2,1,0:T(4,128)(2,1)S(1)} %reshape.381) | copy-start | bytes 393220
  87.1 4.8 %collective-permute-start.1 = (bf16[1,8,4,256]{3,1,2,0:T(8,128)(2,1)S(1)}, bf16[1,8,4,256]{3,1,2,0:T(8,128)(2,1)S(1)}, u32[]{:S(2)}, u32[]{:S(2)}) collective-permute-start(bf16[1,8,4,256]{3,1,2,0:T(8,128)(2,1)S(1)} %copy.153), channel_id=1, source_target_pairs={{64,0},{128,64},{192,128},{256,192},{320,256},{384,320},{448,384},... | collective-permute-start | bytes 49160 | tf_op jit(solution)/shard_map/ppermute | solution.py:23
  90.5 11.0 %copy-start.29 = (bf16[9,8,4,256]{3,1,2,0:T(8,128)(2,1)}, bf16[9,8,4,256]{3,1,2,0:T(8,128)(2,1)S(1)}, u32[]{:S(2)}) copy-start(bf16[9,8,4,256]{3,1,2,0:T(8,128)(2,1)S(1)} %get-tuple-element.53) | copy-start | bytes 442372
  91.8 9.6 %copy-start.23 = (bf16[9,8,4,256]{3,1,2,0:T(8,128)(2,1)}, bf16[9,8,4,256]{3,1,2,0:T(8,128)(2,1)S(1)}, u32[]{:S(2)}) copy-start(bf16[9,8,4,256]{3,1,2,0:T(8,128)(2,1)S(1)} %get-tuple-element.71) | copy-start | bytes 442372
  91.9 9.6 %collective-permute-start.2 = (bf16[10,1,4,256]{3,1,2,0:T(2,128)(2,1)S(1)}, bf16[10,1,4,256]{3,1,2,0:T(2,128)(2,1)S(1)}, u32[]{:S(2)}, u32[]{:S(2)}) collective-permute-start(bf16[10,1,4,256]{3,1,2,0:T(2,128)(2,1)S(1)} %get-tuple-element.50), channel_id=1, source_target_pairs={{0,1},{1,2},{2,3},{3,4},{4,5},{5,6},{6,7},{7,8},{8,9},{9,10},{10,1... | collective-permute-start | bytes 61448 | tf_op jit(solution)/shard_map/ppermute | solution.py:21
  95.1 6.4 %collective-permute-start.3 = (bf16[10,1,4,256]{3,1,2,0:T(2,128)(2,1)S(1)}, bf16[10,1,4,256]{3,1,2,0:T(2,128)(2,1)S(1)}, u32[]{:S(2)}, u32[]{:S(2)}) collective-permute-start(bf16[10,1,4,256]{3,1,2,0:T(2,128)(2,1)S(1)} %get-tuple-element.51), channel_id=1, source_target_pairs={{1,0},{2,1},{3,2},{4,3},{5,4},{6,5},{7,6},{8,7},{9,8},{10,9},{11,1... | collective-permute-start | bytes 61448 | tf_op jit(solution)/shard_map/ppermute | solution.py:23
  101.5 0.6 copy-start.25
  102.1 0.6 copy-start.27
  104.4 0.9 copy-start.26
  104.4 0.9 copy-start.28
  106.4 0.7 copy-start.21
  142.8 1.8 copy-start.30
  145.4 1.8 copy-start.22
  148.1 1.8 copy-start.20
  150.7 1.8 copy-start.16
  153.4 1.8 copy-start.18
  156.1 1.8 copy-start.17
  158.8 1.8 copy-start.24
  161.4 1.8 copy-start.19
  164.9 3.6 copy-start.4
  164.9 4.1 copy-start.5
  164.9 4.3 %copy-start.7 = (bf16[256,256]{1,0:T(8,128)(2,1)S(1)}, bf16[256,256]{1,0:T(8,128)(2,1)}, u32[]{:S(2)}) copy-start(bf16[256,256]{1,0:T(8,128)(2,1)} %reshape.390) | copy-start | bytes 393220
  165.0 4.5 %copy-start.6 = (bf16[256,256]{1,0:T(8,128)(2,1)S(1)}, bf16[256,256]{1,0:T(8,128)(2,1)}, u32[]{:S(2)}) copy-start(bf16[256,256]{1,0:T(8,128)(2,1)} %reshape.391) | copy-start | bytes 393220
  165.0 254.2 %all-reduce.7.cloned.1.call-start = ((), (), s32[]{:S(2)}) async-start(), calls=%async_computation.4 | async-start | bytes 7077888 | tf_op jit(solution)/shard_map/psum | solution.py:10
  165.0 3.7 copy-start.9
  165.0 3.9 copy-start.8
  244.7 13.4 %copy-start.3 = (bf16[8,8,4,256]{3,1,2,0:T(8,128)(2,1)S(1)}, bf16[8,8,4,256]{3,1,2,0:T(8,128)(2,1)}, u32[]{:S(2)}) copy-start(bf16[8,8,4,256]{3,1,2,0:T(8,128)(2,1)} %get-tuple-element.6) | copy-start | bytes 393220
  244.7 15.0 %copy-start.2 = (bf16[8,8,4,256]{3,1,2,0:T(8,128)(2,1)S(1)}, bf16[8,8,4,256]{3,1,2,0:T(8,128)(2,1)}, u32[]{:S(2)}) copy-start(bf16[8,8,4,256]{3,1,2,0:T(8,128)(2,1)} %get-tuple-element.7) | copy-start | bytes 393220
  244.7 16.7 %copy-start.1 = (bf16[8,8,4,256]{3,1,2,0:T(8,128)(2,1)S(1)}, bf16[8,8,4,256]{3,1,2,0:T(8,128)(2,1)}, u32[]{:S(2)}) copy-start(bf16[8,8,4,256]{3,1,2,0:T(8,128)(2,1)} %get-tuple-element.8) | copy-start | bytes 393220
  264.6 5.7 %copy-start.12 = (bf16[256,256]{1,0:T(8,128)(2,1)S(1)}, bf16[256,256]{1,0:T(8,128)(2,1)}, u32[]{:S(2)}) copy-start(bf16[256,256]{1,0:T(8,128)(2,1)} %reshape.397) | copy-start | bytes 393220
  264.6 5.8 %copy-start.14 = (bf16[256,256]{1,0:T(8,128)(2,1)S(1)}, bf16[256,256]{1,0:T(8,128)(2,1)}, u32[]{:S(2)}) copy-start(bf16[256,256]{1,0:T(8,128)(2,1)} %reshape.398) | copy-start | bytes 393220
  266.8 4.1 copy-start.11
  268.0 3.3 copy-start.13
  270.7 1.4 copy-start.10
Sparse Core Ops, SparseCore 0:
  165.1 79.5 all-reduce.4
  248.4 170.7 all-reduce.6
